TPU v7x, 32 devices: a whole 2x2x4 slice. The times are simulated.
32 devices in a mesh: src: 4 (over y, x), tgt: 8 (over z, core).
Axes of the slice: x: 2, y: 2, z: 4, core: 2. Of those that a mesh axis runs over, the one named last changes fastest.
Arguments:
- src_codes: bfloat16 [1024, 6144], P('tgt', 'src'), may hold values from -1 to 1
- src_scale: float32 [6144], P('src'), may hold values from 0.8 to 1.25
- tgt_codes: bfloat16 [1024, 8192], P('src', 'tgt'), may hold values from -1 to 1
- tgt_scale: float32 [8192], P('tgt'), may hold values from 0.8 to 1.25
Outputs:
- forward_best: float32 [4, 6144], P(None, 'src')
- backward_best: float32 [4, 8192], P(None, 'tgt')
All inputs are finite; a program needn't handle non-finite values.
Results may differ from a plain program's by a relative error of at most 0.0003.
Values may be sent and summed in bfloat16 or wider, within the bound.
No kernel may reach another device: no remote copies, remote signals or barrier semaphores. Data moves between devices by JAX's collectives and lax.ppermute only.
A program may use at most 64 MiB of HBM per device.

v0:
```python
import functools
import math

import jax
import jax.numpy as jnp
from jax import lax
from jax.experimental import pallas as pl
from jax.experimental.pallas import tpu as pltpu
from jax.sharding import PartitionSpec as P


TOP = 4
LANES = 128
GROUP = 512
ANY = pl.BlockSpec(memory_space=pl.ANY)
VMEM = pl.BlockSpec(memory_space=pltpu.VMEM)


def params(mib):
    return pltpu.CompilerParams(vmem_limit_bytes=mib << 20)


def exchange(a, b):
    return jnp.maximum(a, b), jnp.minimum(a, b)


def sort4(v):
    a, b, c, d = v
    a, b = exchange(a, b)
    c, d = exchange(c, d)
    a, c = exchange(a, c)
    b, d = exchange(b, d)
    b, c = exchange(b, c)
    return [a, b, c, d]


def merge4(p, q):
    m = [jnp.maximum(p[k], q[TOP - 1 - k]) for k in range(TOP)]
    m[0], m[2] = exchange(m[0], m[2])
    m[1], m[3] = exchange(m[1], m[3])
    m[0], m[1] = exchange(m[0], m[1])
    m[2], m[3] = exchange(m[2], m[3])
    return m


def over_sublanes(lists):
    for shift in (4, 2, 1):
        lists = merge4(lists, [pltpu.roll(x, shift, 0) for x in lists])
    return lists


def sweep_block(load, base, rows, first, lists, state):
    for r in range(0, rows, 32):
        v = [[load(r + 8 * a, b) for b in range(4)] for a in range(4)]
        for b in range(4):
            lists[b] = merge4(lists[b], sort4([v[a][b] for a in range(4)]))
        for a in range(4):
            s = sort4(v[a])
            at = pl.ds(base + (r + 8 * a), 8)
            if not first:
                s = merge4(s, [state[k, at, :] for k in range(TOP)])
            for k in range(TOP):
                state[k, at, :] = s[k]
    return lists


def loop_lists(count, body, write, group):
    def step(q, carried):
        lists = body(q, [list(carried[4 * b : 4 * b + 4]) for b in range(4)])
        return tuple(x for one in lists for x in one)

    empty = tuple(jnp.full((8, LANES), -jnp.inf, jnp.float32) for _ in range(16))
    lists = lax.fori_loop(0, count, step, empty)
    for b in range(4):
        best = over_sublanes(list(lists[4 * b : 4 * b + 4]))
        for k in range(TOP):
            write(k, group * 4 + b, best[k][0:1, :])


def finish_rows(rows, write, state):
    chunks = rows // LANES
    unroll = math.gcd(chunks, 8)

    def one(c):
        x = [state[k, pl.ds(c * LANES, LANES), :].T for k in range(TOP)]
        lists = [[x[k][8 * g : 8 * g + 8, :] for k in range(TOP)] for g in range(LANES // 8)]
        while len(lists) > 1:
            lists = [merge4(lists[i], lists[i + 1]) for i in range(0, len(lists), 2)]
        best = over_sublanes(lists[0])
        for k in range(TOP):
            write(k, c, best[k][0:1, :])

    def body(q, _):
        for h in range(unroll):
            one(q * unroll + h)
        return 0

    lax.fori_loop(0, chunks // unroll, body, 0)


def column_of(row):
    return jnp.broadcast_to(row, (LANES, LANES)).T


def piece_copies(z, core, depth, buf, sem, entries):
    copies = []
    for i, (piece, k, j, h) in enumerate(entries):
        rows = piece.shape[0]
        upward = core == j
        if k == 0:
            block, place, valid = z, jnp.where(upward, 0, 1), None
        else:
            block = jnp.where(upward, z - k, z + k)
            place = jnp.where(upward, h, 1 - h)
            valid = jnp.logical_and(block >= 0, block < depth)
        at = pl.multiple_of((block * 2 + place) * rows, rows)
        copies.append((valid, pltpu.make_async_copy(piece, buf.at[pl.ds(at, rows), :], sem.at[i])))

    def each(act):
        for valid, c in copies:
            if valid is None:
                act(c)
            else:
                pl.when(valid)(functools.partial(act, c))

    return each


def product(targets, sources):
    return lax.dot_general(targets, sources, (((0,), (0,)), ((), ())), preferred_element_type=jnp.float32)


def last_piece(z, core, depth, rows):
    at = pl.multiple_of(jnp.where(z == 0, (depth - 1) * 2 * rows, rows), rows)
    low, high = z == 0, z == depth - 1
    mine = jnp.logical_or(jnp.logical_and(low, core == 1), jnp.logical_and(high, core == 0))
    return at, jnp.logical_or(low, high), mine


def prep_kernel(masks, depth, places, first, *refs):
    n, m = len(masks), len(places)
    tgt, src = refs[:n], refs[n : n + m]
    if first:
        scale_s, scale_t, tgt_buf, src_buf, column, lane, here_s, here_t, tgt_sem, src_sem, scale_sem = refs[n + m :]
    else:
        _, _, tgt_buf, src_buf, part, tgt_sem, src_sem = refs[n + m :]
    t, s = lax.axis_index("tgt"), lax.axis_index("src")
    core, z = t % 2, t // 2
    height = tgt[0].shape[0]
    copies = []
    for i in range(n):
        at = jnp.where(core == 0, s ^ masks[i][0], s ^ masks[i][1]) * height
        copies.append(pltpu.make_async_copy(
            tgt[i], tgt_buf.at[pl.ds(pl.multiple_of(at, height), height), :], tgt_sem.at[i]))
    each = piece_copies(z, core, depth, src_buf, src_sem, [(x, *at) for x, at in zip(src, places)])
    if first:
        scales = [
            pltpu.make_async_copy(scale_s, here_s, scale_sem.at[0]),
            pltpu.make_async_copy(scale_t, here_t, scale_sem.at[1]),
        ]
        for c in scales:
            c.start()
    for c in copies:
        c.start()
    each(lambda c: c.start())
    if first:
        for c in scales:
            c.wait()
        for c in range(column.shape[0] // LANES):
            column[pl.ds(c * LANES, LANES), :] = column_of(here_t[pl.ds(c, 1), :])
        for c in range(lane.shape[1] // LANES):
            lane[:, pl.ds(c * LANES, LANES)] = jnp.broadcast_to(here_s[pl.ds(c, 1), :], (8, LANES))
    for c in copies:
        c.wait()
    each(lambda c: c.wait())
    if not first:
        rows = src[0].shape[0]
        at, missing, _ = last_piece(z, core, depth, rows)

        @pl.when(missing)
        def _():
            src_buf[pl.ds(at, rows), :GROUP] = jnp.zeros((rows, GROUP), src_buf.dtype)

        step = math.gcd(part.shape[0], 256)
        for r in range(0, part.shape[0], step):
            part[pl.ds(r, step), :] = product(tgt_buf[:, pl.ds(r, step)], src_buf[:, :GROUP])


def score_kernel(depth, places, mine_ref, theirs_ref, tgt_buf, _, column, lane, part,
                 src_buf, sim, fwd, bwd, one, two, state, src_sem):
    t = lax.axis_index("tgt")
    core, z = t % 2, t // 2
    sources, targets = src_buf.shape[1], tgt_buf.shape[1]
    each = piece_copies(z, core, depth, src_buf, src_sem,
                        [(x, *at) for x, at in zip((mine_ref, theirs_ref), places)])
    each(lambda c: c.start())
    depth_rows = mine_ref.shape[0]
    slab_at, comes, mine = last_piece(z, core, depth, depth_rows)
    slab = jnp.where(mine, mine_ref[:, :GROUP], theirs_ref[:, :GROUP])
    slab = jnp.where(comes, slab, jnp.zeros_like(slab))
    rows = one.shape[0]
    ns = sources // LANES
    blocks = [(g, r) for g in range(sources // GROUP) for r in range(targets // rows)]

    def dot(g, r, out):
        cols = pl.ds(r * rows, rows)
        if g == 0:
            out[...] = part[cols, :] + product(tgt_buf[pl.ds(slab_at, depth_rows), cols], slab)
        else:
            out[...] = product(tgt_buf[:, cols], src_buf[:, pl.ds(g * GROUP, GROUP)])

    def write_rows(k, c, row):
        bwd[k, pl.ds(c, 1), :] = row

    dot(*blocks[0], one)
    for i, (g, r) in enumerate(blocks):
        now, later = (one, two) if i % 2 == 0 else (two, one)
        if i + 1 < len(blocks):
            if blocks[i + 1] == (1, 0):
                each(lambda c: c.wait())
            dot(*blocks[i + 1], later)

        def load(row, b, now=now, g=g, r=r):
            at, cols = pl.ds(r * rows + row, 8), pl.ds(g * GROUP + LANES * b, LANES)
            v = now[row : row + 8, LANES * b : LANES * (b + 1)] * lane[:, cols] * column[at, :]
            sim[at, cols] = v
            return v

        if r == 0:
            lists = [[jnp.full((8, LANES), -jnp.inf, jnp.float32)] * TOP for _ in range(4)]
        lists = sweep_block(load, r * rows, rows, g == 0, lists, state)
        if r * rows + rows == targets:
            for b in range(4):
                best = over_sublanes(lists[b])
                for k in range(TOP):
                    fwd[pl.ds(k * ns + g * 4 + b, 1), :] = best[k][0:1, :]
    if sources == GROUP:
        each(lambda c: c.wait())
    finish_rows(targets, write_rows, state)


def margin_kernel(sim, fwd_mine, fwd_other, bwd_all, fwd, bwd, column, lane, state):
    targets, sources = sim.shape
    f = merge4(split_list(fwd_mine), split_list(fwd_other))
    f = 0.5 * (0.25 * (f[0] + f[1] + f[2] + f[3]))
    b = 0.5 * (0.25 * (bwd_all[0] + bwd_all[1] + bwd_all[2] + bwd_all[3]))
    for c in range(targets // LANES):
        column[pl.ds(c * LANES, LANES), :] = column_of(b[c : c + 1, :])
    for c in range(sources // LANES):
        lane[:, pl.ds(c * LANES, LANES)] = jnp.broadcast_to(f[c : c + 1, :], (8, LANES))
    rows = math.gcd(targets, 256)

    def write(k, c, row):
        fwd[pl.ds(k * (sources // LANES) + c, 1), :] = row

    def write_rows(k, c, row):
        bwd[k, pl.ds(c, 1), :] = row

    for g in range(sources // GROUP):

        def body(q, lists, g=g):
            base = pl.multiple_of(q * rows, rows)

            def load(row, b):
                at, cols = pl.ds(base + row, 8), pl.ds(g * GROUP + LANES * b, LANES)
                return sim[at, cols] / (lane[:, cols] + column[at, :])

            return sweep_block(load, base, rows, g == 0, lists, state)

        loop_lists(targets // rows, body, write, g)
    finish_rows(targets, write_rows, state)


def split_list(ref):
    n = ref.shape[0] // TOP
    return [ref[n * k : n * (k + 1)] for k in range(TOP)] if len(ref.shape) == 2 else [ref[k] for k in range(TOP)]


def merge_kernel(mine, rec, out):
    merged = merge4(split_list(mine), split_list(rec))
    n = out.shape[0] // TOP
    for k in range(TOP):
        if len(out.shape) == 2:
            out[n * k : n * (k + 1)] = merged[k]
        else:
            out[k] = merged[k]


def final_kernel(fwd_mine, fwd_other, bwd_all, forward, backward):
    f = merge4(split_list(fwd_mine), split_list(fwd_other))
    for k in range(TOP):
        for c in range(forward.shape[1] // LANES):
            forward[pl.ds(k, 1), pl.ds(c * LANES, LANES)] = f[k][c : c + 1, :]
        for c in range(backward.shape[1] // LANES):
            backward[pl.ds(k, 1), pl.ds(c * LANES, LANES)] = bwd_all[k, pl.ds(c, 1), :]


def in_hbm(x):
    return pltpu.with_memory_space_constraint(x, pltpu.HBM)


def f32(*shape):
    return jax.ShapeDtypeStruct(shape, jnp.float32)


def cost(flops, moved):
    return pl.CostEstimate(flops=flops, bytes_accessed=moved, transcendentals=0)


def solution(mesh):
    n_src, n_tgt = mesh.shape["src"], mesh.shape["tgt"]
    depth = n_tgt // 2
    src_bits, z_bits = n_src.bit_length() - 1, depth.bit_length() - 1
    both = ("src", "tgt")

    def flat(s, t):
        return s * n_tgt + t

    devices = [(s, t) for s in range(n_src) for t in range(n_tgt)]
    partner = [(t, t ^ 1) for t in range(n_tgt)]

    def swap(x):
        return lax.ppermute(x, "tgt", partner)

    def along_z(x, step):
        pairs = []
        for t in range(n_tgt):
            z, core = t // 2, t % 2
            if core == 0 and z >= step - 1 and z + 1 < depth:
                pairs.append((t, t + 2))
            if core == 1 and z <= depth - step and z >= 1:
                pairs.append((t, t - 2))
        return lax.ppermute(x, "tgt", pairs)

    def src_masks(step):
        return 1 << step, 1 << (src_bits - 1 - step)

    def along_src(x, masks):
        pairs = [(flat(s, t), flat(s ^ masks[t % 2], t)) for s, t in devices]
        return lax.ppermute(x, both, pairs)

    def merged(mine, rec):
        return pl.pallas_call(
            merge_kernel, out_shape=f32(*mine.shape), in_specs=[VMEM] * 2, out_specs=VMEM,
            compiler_params=params(1), name="merge")(mine, rec)

    def reduce_lists(fwd, bwd):
        for step in range(max(src_bits, z_bits)):
            if step < z_bits:
                pairs = [(t, t ^ (2 << step)) for t in range(n_tgt)]
                from_z = lax.ppermute(fwd, "tgt", pairs)
            if step < src_bits:
                pairs = [(s, s ^ (1 << step)) for s in range(n_src)]
                from_src = lax.ppermute(bwd, "src", pairs)
            if step < z_bits:
                fwd = merged(fwd, from_z)
            if step < src_bits:
                bwd = merged(bwd, from_src)
        return fwd, swap(fwd), bwd

    def compute(src_codes, src_scale, tgt_codes, tgt_scale):
        sources, targets = src_codes.shape[1], tgt_codes.shape[1]
        total = src_codes.shape[0] * n_tgt
        ns, nt = sources // LANES, targets // LANES
        scale_s, scale_t = src_scale.reshape(-1, LANES), tgt_scale.reshape(-1, LANES)

        u, v = src_codes, swap(src_codes)
        own, passed = [(u, (0, 0, 0)), (v, (0, 1, 0))], []
        for step in range(1, depth):
            u = along_z(u, step)
            v = along_z(v, step)
            passed += [(u, (step, 0, 0)), (swap(u), (step, 1, 0)),
                       (v, (step, 0, 1)), (swap(v), (step, 1, 1))]
        passed, late = passed[:-2], passed[-2:]

        held = [(tgt_codes, (0, 0))]
        for step in range(src_bits):
            masks = src_masks(step)
            new = []
            for x, m in held:
                new.append((along_src(x, masks), (m[0] ^ masks[0], m[1] ^ masks[1])))
            held = held + new

        def prep(tgt, src, extra, first):
            shapes = [jax.ShapeDtypeStruct((total, targets), tgt_codes.dtype),
                      jax.ShapeDtypeStruct((total, sources), src_codes.dtype)]
            shapes += [f32(targets, LANES), f32(8, sources)] if first else [f32(targets, GROUP)]
            sems = [pltpu.SemaphoreType.DMA((len(tgt),)), pltpu.SemaphoreType.DMA((len(src),))]
            if first:
                sems = [pltpu.VMEM(scale_s.shape, jnp.float32), pltpu.VMEM(scale_t.shape, jnp.float32)] + sems + [
                    pltpu.SemaphoreType.DMA((2,))]
            count = len(tgt) + len(src)
            return pl.pallas_call(
                functools.partial(prep_kernel, [m for _, m in tgt], depth, [at for _, at in src], first),
                out_shape=shapes, in_specs=[ANY] * count + [ANY if first else VMEM] * 2,
                out_specs=[VMEM] * len(shapes), scratch_shapes=sems,
                input_output_aliases={} if first else {count: 0, count + 1: 1},
                compiler_params=params(4), cost_estimate=cost(0, 4 * total * targets))(*[x for x, _ in tgt], *[x for x, _ in src], *extra)

        tgt_block, src_block, column, lane = prep(
            [(in_hbm(tgt_codes), (0, 0))] + held[1:-1], [(in_hbm(src_codes), own[0][1]), own[1]] + passed[:-6],
            (in_hbm(scale_s), in_hbm(scale_t)), True)
        tgt_block, src_block, part = prep(held[-1:], passed[-6:], (tgt_block, src_block), False)
        block = min(512, targets // 2)
        _, sim, fwd, bwd = pl.pallas_call(
            functools.partial(score_kernel, depth, [at for _, at in late]),
            out_shape=(jax.ShapeDtypeStruct((total, sources), src_codes.dtype),
                       f32(targets, sources), f32(TOP * ns, LANES), f32(TOP, nt, LANES)),
            in_specs=[VMEM] * 7, out_specs=(VMEM,) * 4,
            input_output_aliases={3: 0},
            scratch_shapes=[
                pltpu.VMEM((block, GROUP), jnp.float32),
                pltpu.VMEM((block, GROUP), jnp.float32),
                pltpu.VMEM((TOP, targets, LANES), jnp.float32),
                pltpu.SemaphoreType.DMA((2,)),
            ],
            compiler_params=params(8), cost_estimate=cost(2 * total * sources * targets, 4 * sources * targets),
            name="score")(*[x for x, _ in late], tgt_block, src_block, column, lane, part)

        fwd, bwd = pl.pallas_call(
            margin_kernel,
            out_shape=(f32(TOP * ns, LANES), f32(TOP, nt, LANES)),
            in_specs=[VMEM] * 4, out_specs=(VMEM,) * 2,
            scratch_shapes=[
                pltpu.VMEM((targets, LANES), jnp.float32),
                pltpu.VMEM((8, sources), jnp.float32),
                pltpu.VMEM((TOP, targets, LANES), jnp.float32),
            ],
            compiler_params=params(8), cost_estimate=cost(30 * sources * targets, 4 * sources * targets),
            name="margin")(sim, *reduce_lists(fwd, bwd))
        return pl.pallas_call(
            final_kernel, out_shape=(f32(TOP, sources), f32(TOP, targets)),
            in_specs=[VMEM] * 3, out_specs=(VMEM,) * 2, compiler_params=params(1),
            name="final")(*reduce_lists(fwd, bwd))

    placed = (P("tgt", "src"), P("src"), P("src", "tgt"), P("tgt"))
    return jax.shard_map(
        compute, mesh=mesh, in_specs=placed, out_specs=(P(None, "src"), P(None, "tgt")), check_vma=False)
```

profile of v0, /device:TPU:0, one launch (start us, length us, event | category | flops | bytes accessed | tf_op | source)
XLA Modules:
  0.0 76.5 jit_solution(4385916977996614653)
XLA Ops:
  1.2 4.5 %collective-permute-start.7 = (bf16[128,1536]{1,0:T(8,128)(2,1)}, bf16[128,1536]{1,0:T(8,128)(2,1)S(1)}, u32[]{:S(2)}, u32[]{:S(2)}) collective-permute-start(bf16[128,1536]{1,0:T(8,128)(2,1)} %refs_3_.1), channel_id=1, source_target_pairs={{0,2},{2,4},{3,1},{4,6},{5,3},{7,5},{8,10},{10,12},{11,9},{12,14},... | collective-permute-start | bytes 1179656 | tf_op jit(solution)/shard_map/ppermute | solution.py:333
  5.7 3.5 %collective-permute-start.1 = (bf16[128,1536]{1,0:T(8,128)(2,1)S(1)}, bf16[128,1536]{1,0:T(8,128)(2,1)S(1)}, u32[]{:S(2)}, u32[]{:S(2)}) collective-permute-start(bf16[128,1536]{1,0:T(8,128)(2,1)S(1)} %collective-permute-done.refs_4_), channel_id=1, source_target_pairs={{0,2},{2,4},{3,1},{4,6},{5,3},{7,5},{8,10},{10,12},{11,9},{12,14},... | collective-permute-start | bytes 1179656 | tf_op jit(solution)/shard_map/ppermute | solution.py:333
  9.2 1.6 %collective-permute-start.5 = (bf16[256,1024]{1,0:T(8,128)(2,1)}, bf16[256,1024]{1,0:T(8,128)(2,1)S(1)}, u32[]{:S(2)}, u32[]{:S(2)}) collective-permute-start(bf16[256,1024]{1,0:T(8,128)(2,1)} %refs_0_.1), channel_id=1, source_target_pairs={{0,8},{1,17},{2,10},{3,19},{4,12},{5,21},{6,14},{7,23},{8,0},{9,25... | collective-permute-start | bytes 1572872 | tf_op jit(solution)/shard_map/ppermute | solution.py:340
  11.3 0.7 collective-permute-start.8
  11.9 3.4 %collective-permute-done.1.refs_7_ = bf16[128,1536]{1,0:T(8,128)(2,1)S(1)} collective-permute-done((bf16[128,1536]{1,0:T(8,128)(2,1)S(1)}, bf16[128,1536]{1,0:T(8,128)(2,1)S(1)}, u32[]{:S(2)}, u32[]{:S(2)}) %collective-permute-start.1) | collective-permute-done | bytes 393248 | tf_op jit(solution)/shard_map/ppermute | solution.py:333
  15.4 0.7 collective-permute-start.2
  16.1 1.6 %collective-permute-start.13 = (bf16[256,1024]{1,0:T(8,128)(2,1)}, bf16[256,1024]{1,0:T(8,128)(2,1)S(1)}, u32[]{:S(2)}, u32[]{:S(2)}) collective-permute-start(bf16[256,1024]{1,0:T(8,128)(2,1)} %refs_0_.1), channel_id=1, source_target_pairs={{0,16},{1,9},{2,18},{3,11},{4,20},{5,13},{6,22},{7,15},{8,24},{9,1... | collective-permute-start | bytes 1572872 | tf_op jit(solution)/shard_map/ppermute | solution.py:340
  17.6 0.8 %collective-permute-start.14 = (bf16[128,1536]{1,0:T(8,128)(2,1)S(1)}, bf16[128,1536]{1,0:T(8,128)(2,1)S(1)}, u32[]{:S(2)}, u32[]{:S(2)}) collective-permute-start(bf16[128,1536]{1,0:T(8,128)(2,1)S(1)} %collective-permute-done.7.refs_5_), channel_id=1, source_target_pairs={{0,1},{1,0},{2,3},{3,2},{4,5},{5,4},{6,7},{7,6},{8,9},{9,8},{10,11... | collective-permute-start | bytes 1179656 | tf_op jit(solution)/shard_map/ppermute | solution.py:323
  18.7 0.7 collective-permute-start.11
  19.4 0.7 collective-permute-start.3
  20.1 5.5 %collective-permute-done.13.refs_2_ = bf16[256,1024]{1,0:T(8,128)(2,1)S(1)} collective-permute-done((bf16[256,1024]{1,0:T(8,128)(2,1)}, bf16[256,1024]{1,0:T(8,128)(2,1)S(1)}, u32[]{:S(2)}, u32[]{:S(2)}) %collective-permute-start.13) | collective-permute-done | bytes 524320 | tf_op jit(solution)/shard_map/ppermute | solution.py:340
  25.5 1.5 %collective-permute-start.6 = (bf16[256,1024]{1,0:T(8,128)(2,1)S(1)}, bf16[256,1024]{1,0:T(8,128)(2,1)S(1)}, u32[]{:S(2)}, u32[]{:S(2)}) collective-permute-start(bf16[256,1024]{1,0:T(8,128)(2,1)S(1)} %collective-permute-done.5.refs_1_), channel_id=1, source_target_pairs={{0,16},{1,9},{2,18},{3,11},{4,20},{5,13},{6,22},{7,15},{8,24},{9,1... | collective-permute-start | bytes 1572872 | tf_op jit(solution)/shard_map/ppermute | solution.py:340
  27.6 2.4 %collective-permute-start.12 = (bf16[128,1536]{1,0:T(8,128)(2,1)S(1)}, bf16[128,1536]{1,0:T(8,128)(2,1)S(1)}, u32[]{:S(2)}, u32[]{:S(2)}) collective-permute-start(bf16[128,1536]{1,0:T(8,128)(2,1)S(1)} %collective-permute-done.11.refs_5_), channel_id=1, source_target_pairs={{0,1},{1,0},{2,3},{3,2},{4,5},{5,4},{6,7},{7,6},{8,9},{9,8},{10,11... | collective-permute-start | bytes 1179656 | tf_op jit(solution)/shard_map/ppermute | solution.py:323
  29.9 4.2 %collective-permute-start.4 = (bf16[128,1536]{1,0:T(8,128)(2,1)S(1)}, bf16[128,1536]{1,0:T(8,128)(2,1)S(1)}, u32[]{:S(2)}, u32[]{:S(2)}) collective-permute-start(bf16[128,1536]{1,0:T(8,128)(2,1)S(1)} %collective-permute-done.3.mine_ref), channel_id=1, source_target_pairs={{0,1},{1,0},{2,3},{3,2},{4,5},{5,4},{6,7},{7,6},{8,9},{9,8},{10,11... | collective-permute-start | bytes 1179656 | tf_op jit(solution)/shard_map/ppermute | solution.py:323
  34.1 1.3 %shard_map.59 = (bf16[1024,1024]{1,0:T(8,128)(2,1)S(1)}, bf16[1024,1536]{1,0:T(8,128)(2,1)S(1)}, f32[1024,128]{1,0:T(8,128)S(1)}, f32[8,1536]{1,0:T(8,128)S(1)}) custom-call(bf16[256,1024]{1,0:T(8,128)(2,1)} %refs_0_.1, bf16[256,1024]{1,0:T(8,128)(2,1)S(1)} %collective-permute-done.5.refs_1_, bf16[256,1024]{1,0:T(8,128)(2,1)S(1)} %collective-permute-done.13.refs_2_, ...), custom_call_target="tpu_custom_call" | custom-call | bytes 4194304 | tf_op jit(solution)/shard_map/pallas_call | solution.py:393
  35.5 2.1 %shard_map.60 = (bf16[1024,1024]{1,0:T(8,128)(2,1)S(1)}, bf16[1024,1536]{1,0:T(8,128)(2,1)S(1)}, f32[1024,512]{1,0:T(8,128)S(1)}) custom-call(bf16[256,1024]{1,0:T(8,128)(2,1)S(1)} %collective-permute-done.6.refs_0_, bf16[128,1536]{1,0:T(8,128)(2,1)S(1)} %collective-permute-done.8.refs_1_, ...), custom_call_target="tpu_custom_call", output_to_operand_aliasing={{0}: (7, {}), {1}: (8, {})} | custom-call | bytes 4194304 | tf_op jit(solution)/shard_map/pallas_call | solution.py:393
  37.6 5.0 %score.1 = (bf16[1024,1536]{1,0:T(8,128)(2,1)S(1)}, f32[1024,1536]{1,0:T(8,128)S(1)}, f32[48,128]{1,0:T(8,128)S(1)}, f32[4,8,128]{2,1,0:T(8,128)S(1)}) custom-call(bf16[128,1536]{1,0:T(8,128)(2,1)S(1)} %collective-permute-done.3.mine_ref, bf16[128,1536]{1,0:T(8,128)(2,1)S(1)} %collective-permute-done.4.theirs_ref, ...), custom_call_target="tpu_custom_call", output_to_operand_aliasing={{0}: (3, {})} | custom-call | flops 3221225472 | bytes 6291456 | tf_op jit(solution)/shard_map/score/pallas_call | solution.py:405
  42.5 4.2 %collective-permute-start.16 = (f32[48,128]{1,0:T(8,128)S(1)}, f32[48,128]{1,0:T(8,128)S(1)}, u32[]{:S(2)}, u32[]{:S(2)}) collective-permute-start(f32[48,128]{1,0:T(8,128)S(1)} %get-tuple-element.22.mine), channel_id=1, source_target_pairs={{0,2},{1,3},{2,0},{3,1},{4,6},{5,7},{6,4},{7,5},{8,10},{9,11},{10,... | collective-permute-start | bytes 73736 | tf_op jit(solution)/shard_map/ppermute | solution.py:351
  46.7 1.8 %collective-permute-done.16.rec = f32[48,128]{1,0:T(8,128)S(1)} collective-permute-done((f32[48,128]{1,0:T(8,128)S(1)}, f32[48,128]{1,0:T(8,128)S(1)}, u32[]{:S(2)}, u32[]{:S(2)}) %collective-permute-start.16) | collective-permute-done | bytes 24608 | tf_op jit(solution)/shard_map/ppermute | solution.py:351
  48.5 3.4 %collective-permute-start.17 = (f32[48,128]{1,0:T(8,128)S(1)}, f32[48,128]{1,0:T(8,128)S(1)}, u32[]{:S(2)}, u32[]{:S(2)}) collective-permute-start(f32[48,128]{1,0:T(8,128)S(1)} %merge.8.mine), channel_id=1, source_target_pairs={{0,4},{1,5},{2,6},{3,7},{4,0},{5,1},{6,2},{7,3},{8,12},{9,13},{10,... | collective-permute-start | bytes 73736 | tf_op jit(solution)/shard_map/ppermute | solution.py:351
  51.9 1.5 %collective-permute-start.19 = (f32[4,8,128]{2,1,0:T(8,128)S(1)}, f32[4,8,128]{2,1,0:T(8,128)S(1)}, u32[]{:S(2)}, u32[]{:S(2)}) collective-permute-start(f32[4,8,128]{2,1,0:T(8,128)S(1)} %get-tuple-element.23.mine), channel_id=1, source_target_pairs={{0,8},{8,0},{16,24},{24,16},{1,9},{9,1},{17,25},{25,17},{2,10},{10... | collective-permute-start | bytes 49160 | tf_op jit(solution)/shard_map/ppermute | solution.py:354
  53.8 1.8 %collective-permute-done.19.rec = f32[4,8,128]{2,1,0:T(8,128)S(1)} collective-permute-done((f32[4,8,128]{2,1,0:T(8,128)S(1)}, f32[4,8,128]{2,1,0:T(8,128)S(1)}, u32[]{:S(2)}, u32[]{:S(2)}) %collective-permute-start.19) | collective-permute-done | bytes 16416 | tf_op jit(solution)/shard_map/ppermute | solution.py:354
  55.7 1.5 %collective-permute-start.20 = (f32[4,8,128]{2,1,0:T(8,128)S(1)}, f32[4,8,128]{2,1,0:T(8,128)S(1)}, u32[]{:S(2)}, u32[]{:S(2)}) collective-permute-start(f32[4,8,128]{2,1,0:T(8,128)S(1)} %merge.10.mine), channel_id=1, source_target_pairs={{0,16},{8,24},{16,0},{24,8},{1,17},{9,25},{17,1},{25,9},{2,18},{10... | collective-permute-start | bytes 49160 | tf_op jit(solution)/shard_map/ppermute | solution.py:354
  57.2 2.2 %collective-permute-done.20.rec = f32[4,8,128]{2,1,0:T(8,128)S(1)} collective-permute-done((f32[4,8,128]{2,1,0:T(8,128)S(1)}, f32[4,8,128]{2,1,0:T(8,128)S(1)}, u32[]{:S(2)}, u32[]{:S(2)}) %collective-permute-start.20) | collective-permute-done | bytes 16416 | tf_op jit(solution)/shard_map/ppermute | solution.py:354
  59.4 3.8 %margin.1 = (f32[48,128]{1,0:T(8,128)S(1)}, f32[4,8,128]{2,1,0:T(8,128)S(1)}) custom-call(f32[1024,1536]{1,0:T(8,128)S(1)} %get-tuple-element.21.sim, f32[48,128]{1,0:T(8,128)S(1)} %merge.9.fwd_mine, f32[48,128]{1,0:T(8,128)S(1)} %collective-permute-done.18.fwd_other, f32[4,8,128]{2,1,0:T(8,128)S(1)} %merge.11.bwd_all), custom_call_target="tpu_custom_call" | custom-call | flops 47185920 | bytes 6291456 | tf_op jit(solution)/shard_map/margin/pallas_call | solution.py:420
  63.4 3.6 %collective-permute-done.21.rec = f32[48,128]{1,0:T(8,128)S(1)} collective-permute-done((f32[48,128]{1,0:T(8,128)S(1)}, f32[48,128]{1,0:T(8,128)S(1)}, u32[]{:S(2)}, u32[]{:S(2)}) %collective-permute-start.21) | collective-permute-done | bytes 24608 | tf_op jit(solution)/shard_map/ppermute | solution.py:351
  67.1 1.2 %collective-permute-start.22 = (f32[48,128]{1,0:T(8,128)S(1)}, f32[48,128]{1,0:T(8,128)S(1)}, u32[]{:S(2)}, u32[]{:S(2)}) collective-permute-start(f32[48,128]{1,0:T(8,128)S(1)} %merge.12.mine), channel_id=1, source_target_pairs={{0,4},{1,5},{2,6},{3,7},{4,0},{5,1},{6,2},{7,3},{8,12},{9,13},{10,... | collective-permute-start | bytes 73736 | tf_op jit(solution)/shard_map/ppermute | solution.py:351
  68.3 1.5 %collective-permute-start.24 = (f32[4,8,128]{2,1,0:T(8,128)S(1)}, f32[4,8,128]{2,1,0:T(8,128)S(1)}, u32[]{:S(2)}, u32[]{:S(2)}) collective-permute-start(f32[4,8,128]{2,1,0:T(8,128)S(1)} %get-tuple-element.25.mine), channel_id=1, source_target_pairs={{0,8},{8,0},{16,24},{24,16},{1,9},{9,1},{17,25},{25,17},{2,10},{10... | collective-permute-start | bytes 49160 | tf_op jit(solution)/shard_map/ppermute | solution.py:354
  69.8 2.1 %collective-permute-done.22.rec = f32[48,128]{1,0:T(8,128)S(1)} collective-permute-done((f32[48,128]{1,0:T(8,128)S(1)}, f32[48,128]{1,0:T(8,128)S(1)}, u32[]{:S(2)}, u32[]{:S(2)}) %collective-permute-start.22) | collective-permute-done | bytes 24608 | tf_op jit(solution)/shard_map/ppermute | solution.py:351
  72.1 1.5 %collective-permute-start.25 = (f32[4,8,128]{2,1,0:T(8,128)S(1)}, f32[4,8,128]{2,1,0:T(8,128)S(1)}, u32[]{:S(2)}, u32[]{:S(2)}) collective-permute-start(f32[4,8,128]{2,1,0:T(8,128)S(1)} %merge.14.mine), channel_id=1, source_target_pairs={{0,16},{8,24},{16,0},{24,8},{1,17},{9,25},{17,1},{25,9},{2,18},{10... | collective-permute-start | bytes 49160 | tf_op jit(solution)/shard_map/ppermute | solution.py:354
  73.6 2.2 %collective-permute-done.25.rec = f32[4,8,128]{2,1,0:T(8,128)S(1)} collective-permute-done((f32[4,8,128]{2,1,0:T(8,128)S(1)}, f32[4,8,128]{2,1,0:T(8,128)S(1)}, u32[]{:S(2)}, u32[]{:S(2)}) %collective-permute-start.25) | collective-permute-done | bytes 16416 | tf_op jit(solution)/shard_map/ppermute | solution.py:354
  75.8 0.6 final.1
  (33 shorter events, 2.7 us)
Async XLA Ops:
  0.6 5.1 %collective-permute-start = (bf16[128,1536]{1,0:T(8,128)(2,1)}, bf16[128,1536]{1,0:T(8,128)(2,1)S(1)}, u32[]{:S(2)}, u32[]{:S(2)}) collective-permute-start(bf16[128,1536]{1,0:T(8,128)(2,1)} %refs_3_.1), channel_id=1, source_target_pairs={{0,1},{1,0},{2,3},{3,2},{4,5},{5,4},{6,7},{7,6},{8,9},{9,8},{10,11... | collective-permute-start | bytes 1179656 | tf_op jit(solution)/shard_map/ppermute | solution.py:323
  1.2 10.1 %collective-permute-start.7 = (bf16[128,1536]{1,0:T(8,128)(2,1)}, bf16[128,1536]{1,0:T(8,128)(2,1)S(1)}, u32[]{:S(2)}, u32[]{:S(2)}) collective-permute-start(bf16[128,1536]{1,0:T(8,128)(2,1)} %refs_3_.1), channel_id=1, source_target_pairs={{0,2},{2,4},{3,1},{4,6},{5,3},{7,5},{8,10},{10,12},{11,9},{12,14},... | collective-permute-start | bytes 1179656 | tf_op jit(solution)/shard_map/ppermute | solution.py:333
  5.7 9.7 %collective-permute-start.1 = (bf16[128,1536]{1,0:T(8,128)(2,1)S(1)}, bf16[128,1536]{1,0:T(8,128)(2,1)S(1)}, u32[]{:S(2)}, u32[]{:S(2)}) collective-permute-start(bf16[128,1536]{1,0:T(8,128)(2,1)S(1)} %collective-permute-done.refs_4_), channel_id=1, source_target_pairs={{0,2},{2,4},{3,1},{4,6},{5,3},{7,5},{8,10},{10,12},{11,9},{12,14},... | collective-permute-start | bytes 1179656 | tf_op jit(solution)/shard_map/ppermute | solution.py:333
  9.2 9.5 %collective-permute-start.5 = (bf16[256,1024]{1,0:T(8,128)(2,1)}, bf16[256,1024]{1,0:T(8,128)(2,1)S(1)}, u32[]{:S(2)}, u32[]{:S(2)}) collective-permute-start(bf16[256,1024]{1,0:T(8,128)(2,1)} %refs_0_.1), channel_id=1, source_target_pairs={{0,8},{1,17},{2,10},{3,19},{4,12},{5,21},{6,14},{7,23},{8,0},{9,25... | collective-permute-start | bytes 1572872 | tf_op jit(solution)/shard_map/ppermute | solution.py:340
  11.3 7.4 %collective-permute-start.8 = (bf16[128,1536]{1,0:T(8,128)(2,1)S(1)}, bf16[128,1536]{1,0:T(8,128)(2,1)S(1)}, u32[]{:S(2)}, u32[]{:S(2)}) collective-permute-start(bf16[128,1536]{1,0:T(8,128)(2,1)S(1)} %collective-permute-done.7.refs_5_), channel_id=1, source_target_pairs={{2,4},{3,1},{4,6},{5,3},{10,12},{11,9},{12,14},{13,11},{18,20},{19... | collective-permute-start | bytes 1179656 | tf_op jit(solution)/shard_map/ppermute | solution.py:333
  15.4 4.0 %collective-permute-start.2 = (bf16[128,1536]{1,0:T(8,128)(2,1)S(1)}, bf16[128,1536]{1,0:T(8,128)(2,1)S(1)}, u32[]{:S(2)}, u32[]{:S(2)}) collective-permute-start(bf16[128,1536]{1,0:T(8,128)(2,1)S(1)} %collective-permute-done.1.refs_7_), channel_id=1, source_target_pairs={{2,4},{3,1},{4,6},{5,3},{10,12},{11,9},{12,14},{13,11},{18,20},{19... | collective-permute-start | bytes 1179656 | tf_op jit(solution)/shard_map/ppermute | solution.py:333
  16.1 9.5 %collective-permute-start.13 = (bf16[256,1024]{1,0:T(8,128)(2,1)}, bf16[256,1024]{1,0:T(8,128)(2,1)S(1)}, u32[]{:S(2)}, u32[]{:S(2)}) collective-permute-start(bf16[256,1024]{1,0:T(8,128)(2,1)} %refs_0_.1), channel_id=1, source_target_pairs={{0,16},{1,9},{2,18},{3,11},{4,20},{5,13},{6,22},{7,15},{8,24},{9,1... | collective-permute-start | bytes 1572872 | tf_op jit(solution)/shard_map/ppermute | solution.py:340
  17.6 9.4 %collective-permute-start.14 = (bf16[128,1536]{1,0:T(8,128)(2,1)S(1)}, bf16[128,1536]{1,0:T(8,128)(2,1)S(1)}, u32[]{:S(2)}, u32[]{:S(2)}) collective-permute-start(bf16[128,1536]{1,0:T(8,128)(2,1)S(1)} %collective-permute-done.7.refs_5_), channel_id=1, source_target_pairs={{0,1},{1,0},{2,3},{3,2},{4,5},{5,4},{6,7},{7,6},{8,9},{9,8},{10,11... | collective-permute-start | bytes 1179656 | tf_op jit(solution)/shard_map/ppermute | solution.py:323
  18.7 8.6 %collective-permute-start.15 = (bf16[128,1536]{1,0:T(8,128)(2,1)S(1)}, bf16[128,1536]{1,0:T(8,128)(2,1)S(1)}, u32[]{:S(2)}, u32[]{:S(2)}) collective-permute-start(bf16[128,1536]{1,0:T(8,128)(2,1)S(1)} %collective-permute-done.1.refs_7_), channel_id=1, source_target_pairs={{0,1},{1,0},{2,3},{3,2},{4,5},{5,4},{6,7},{7,6},{8,9},{9,8},{10,11... | collective-permute-start | bytes 1179656 | tf_op jit(solution)/shard_map/ppermute | solution.py:323
  18.7 8.9 %collective-permute-start.11 = (bf16[128,1536]{1,0:T(8,128)(2,1)S(1)}, bf16[128,1536]{1,0:T(8,128)(2,1)S(1)}, u32[]{:S(2)}, u32[]{:S(2)}) collective-permute-start(bf16[128,1536]{1,0:T(8,128)(2,1)S(1)} %collective-permute-done.8.refs_1_), channel_id=1, source_target_pairs={{3,1},{4,6},{11,9},{12,14},{19,17},{20,22},{27,25},{28,30}} | collective-permute-start | bytes 1179656 | tf_op jit(solution)/shard_map/ppermute | solution.py:333
  19.4 10.6 %collective-permute-start.3 = (bf16[128,1536]{1,0:T(8,128)(2,1)S(1)}, bf16[128,1536]{1,0:T(8,128)(2,1)S(1)}, u32[]{:S(2)}, u32[]{:S(2)}) collective-permute-start(bf16[128,1536]{1,0:T(8,128)(2,1)S(1)} %collective-permute-done.2.refs_3_), channel_id=1, source_target_pairs={{3,1},{4,6},{11,9},{12,14},{19,17},{20,22},{27,25},{28,30}} | collective-permute-start | bytes 1179656 | tf_op jit(solution)/shard_map/ppermute | solution.py:333
  25.5 9.9 %collective-permute-start.6 = (bf16[256,1024]{1,0:T(8,128)(2,1)S(1)}, bf16[256,1024]{1,0:T(8,128)(2,1)S(1)}, u32[]{:S(2)}, u32[]{:S(2)}) collective-permute-start(bf16[256,1024]{1,0:T(8,128)(2,1)S(1)} %collective-permute-done.5.refs_1_), channel_id=1, source_target_pairs={{0,16},{1,9},{2,18},{3,11},{4,20},{5,13},{6,22},{7,15},{8,24},{9,1... | collective-permute-start | bytes 1572872 | tf_op jit(solution)/shard_map/ppermute | solution.py:340
  27.0 8.4 %collective-permute-start.9 = (bf16[128,1536]{1,0:T(8,128)(2,1)S(1)}, bf16[128,1536]{1,0:T(8,128)(2,1)S(1)}, u32[]{:S(2)}, u32[]{:S(2)}) collective-permute-start(bf16[128,1536]{1,0:T(8,128)(2,1)S(1)} %collective-permute-done.8.refs_1_), channel_id=1, source_target_pairs={{0,1},{1,0},{2,3},{3,2},{4,5},{5,4},{6,7},{7,6},{8,9},{9,8},{10,11... | collective-permute-start | bytes 1179656 | tf_op jit(solution)/shard_map/ppermute | solution.py:323
  27.3 8.2 %collective-permute-start.10 = (bf16[128,1536]{1,0:T(8,128)(2,1)S(1)}, bf16[128,1536]{1,0:T(8,128)(2,1)S(1)}, u32[]{:S(2)}, u32[]{:S(2)}) collective-permute-start(bf16[128,1536]{1,0:T(8,128)(2,1)S(1)} %collective-permute-done.2.refs_3_), channel_id=1, source_target_pairs={{0,1},{1,0},{2,3},{3,2},{4,5},{5,4},{6,7},{7,6},{8,9},{9,8},{10,11... | collective-permute-start | bytes 1179656 | tf_op jit(solution)/shard_map/ppermute | solution.py:323
  27.6 7.9 %collective-permute-start.12 = (bf16[128,1536]{1,0:T(8,128)(2,1)S(1)}, bf16[128,1536]{1,0:T(8,128)(2,1)S(1)}, u32[]{:S(2)}, u32[]{:S(2)}) collective-permute-start(bf16[128,1536]{1,0:T(8,128)(2,1)S(1)} %collective-permute-done.11.refs_5_), channel_id=1, source_target_pairs={{0,1},{1,0},{2,3},{3,2},{4,5},{5,4},{6,7},{7,6},{8,9},{9,8},{10,11... | collective-permute-start | bytes 1179656 | tf_op jit(solution)/shard_map/ppermute | solution.py:323
  29.9 7.6 %collective-permute-start.4 = (bf16[128,1536]{1,0:T(8,128)(2,1)S(1)}, bf16[128,1536]{1,0:T(8,128)(2,1)S(1)}, u32[]{:S(2)}, u32[]{:S(2)}) collective-permute-start(bf16[128,1536]{1,0:T(8,128)(2,1)S(1)} %collective-permute-done.3.mine_ref), channel_id=1, source_target_pairs={{0,1},{1,0},{2,3},{3,2},{4,5},{5,4},{6,7},{7,6},{8,9},{9,8},{10,11... | collective-permute-start | bytes 1179656 | tf_op jit(solution)/shard_map/ppermute | solution.py:323
  42.5 6.0 %collective-permute-start.16 = (f32[48,128]{1,0:T(8,128)S(1)}, f32[48,128]{1,0:T(8,128)S(1)}, u32[]{:S(2)}, u32[]{:S(2)}) collective-permute-start(f32[48,128]{1,0:T(8,128)S(1)} %get-tuple-element.22.mine), channel_id=1, source_target_pairs={{0,2},{1,3},{2,0},{3,1},{4,6},{5,7},{6,4},{7,5},{8,10},{9,11},{10,... | collective-permute-start | bytes 73736 | tf_op jit(solution)/shard_map/ppermute | solution.py:351
  48.5 5.2 %collective-permute-start.17 = (f32[48,128]{1,0:T(8,128)S(1)}, f32[48,128]{1,0:T(8,128)S(1)}, u32[]{:S(2)}, u32[]{:S(2)}) collective-permute-start(f32[48,128]{1,0:T(8,128)S(1)} %merge.8.mine), channel_id=1, source_target_pairs={{0,4},{1,5},{2,6},{3,7},{4,0},{5,1},{6,2},{7,3},{8,12},{9,13},{10,... | collective-permute-start | bytes 73736 | tf_op jit(solution)/shard_map/ppermute | solution.py:351
  51.9 3.7 %collective-permute-start.19 = (f32[4,8,128]{2,1,0:T(8,128)S(1)}, f32[4,8,128]{2,1,0:T(8,128)S(1)}, u32[]{:S(2)}, u32[]{:S(2)}) collective-permute-start(f32[4,8,128]{2,1,0:T(8,128)S(1)} %get-tuple-element.23.mine), channel_id=1, source_target_pairs={{0,8},{8,0},{16,24},{24,16},{1,9},{9,1},{17,25},{25,17},{2,10},{10... | collective-permute-start | bytes 49160 | tf_op jit(solution)/shard_map/ppermute | solution.py:354
  53.7 5.7 %collective-permute-start.18 = (f32[48,128]{1,0:T(8,128)S(1)}, f32[48,128]{1,0:T(8,128)S(1)}, u32[]{:S(2)}, u32[]{:S(2)}) collective-permute-start(f32[48,128]{1,0:T(8,128)S(1)} %merge.9.fwd_mine), channel_id=1, source_target_pairs={{0,1},{1,0},{2,3},{3,2},{4,5},{5,4},{6,7},{7,6},{8,9},{9,8},{10,11... | collective-permute-start | bytes 73736 | tf_op jit(solution)/shard_map/ppermute | solution.py:323
  55.7 3.7 %collective-permute-start.20 = (f32[4,8,128]{2,1,0:T(8,128)S(1)}, f32[4,8,128]{2,1,0:T(8,128)S(1)}, u32[]{:S(2)}, u32[]{:S(2)}) collective-permute-start(f32[4,8,128]{2,1,0:T(8,128)S(1)} %merge.10.mine), channel_id=1, source_target_pairs={{0,16},{8,24},{16,0},{24,8},{1,17},{9,25},{17,1},{25,9},{2,18},{10... | collective-permute-start | bytes 49160 | tf_op jit(solution)/shard_map/ppermute | solution.py:354
  63.2 3.9 %collective-permute-start.21 = (f32[48,128]{1,0:T(8,128)S(1)}, f32[48,128]{1,0:T(8,128)S(1)}, u32[]{:S(2)}, u32[]{:S(2)}) collective-permute-start(f32[48,128]{1,0:T(8,128)S(1)} %get-tuple-element.24.mine), channel_id=1, source_target_pairs={{0,2},{1,3},{2,0},{3,1},{4,6},{5,7},{6,4},{7,5},{8,10},{9,11},{10,... | collective-permute-start | bytes 73736 | tf_op jit(solution)/shard_map/ppermute | solution.py:351
  67.1 4.8 %collective-permute-start.22 = (f32[48,128]{1,0:T(8,128)S(1)}, f32[48,128]{1,0:T(8,128)S(1)}, u32[]{:S(2)}, u32[]{:S(2)}) collective-permute-start(f32[48,128]{1,0:T(8,128)S(1)} %merge.12.mine), channel_id=1, source_target_pairs={{0,4},{1,5},{2,6},{3,7},{4,0},{5,1},{6,2},{7,3},{8,12},{9,13},{10,... | collective-permute-start | bytes 73736 | tf_op jit(solution)/shard_map/ppermute | solution.py:351
  68.3 3.7 %collective-permute-start.24 = (f32[4,8,128]{2,1,0:T(8,128)S(1)}, f32[4,8,128]{2,1,0:T(8,128)S(1)}, u32[]{:S(2)}, u32[]{:S(2)}) collective-permute-start(f32[4,8,128]{2,1,0:T(8,128)S(1)} %get-tuple-element.25.mine), channel_id=1, source_target_pairs={{0,8},{8,0},{16,24},{24,16},{1,9},{9,1},{17,25},{25,17},{2,10},{10... | collective-permute-start | bytes 49160 | tf_op jit(solution)/shard_map/ppermute | solution.py:354
  71.9 3.9 %collective-permute-start.23 = (f32[48,128]{1,0:T(8,128)S(1)}, f32[48,128]{1,0:T(8,128)S(1)}, u32[]{:S(2)}, u32[]{:S(2)}) collective-permute-start(f32[48,128]{1,0:T(8,128)S(1)} %merge.13.fwd_mine), channel_id=1, source_target_pairs={{0,1},{1,0},{2,3},{3,2},{4,5},{5,4},{6,7},{7,6},{8,9},{9,8},{10,11... | collective-permute-start | bytes 73736 | tf_op jit(solution)/shard_map/ppermute | solution.py:323
  72.1 3.7 %collective-permute-start.25 = (f32[4,8,128]{2,1,0:T(8,128)S(1)}, f32[4,8,128]{2,1,0:T(8,128)S(1)}, u32[]{:S(2)}, u32[]{:S(2)}) collective-permute-start(f32[4,8,128]{2,1,0:T(8,128)S(1)} %merge.14.mine), channel_id=1, source_target_pairs={{0,16},{8,24},{16,0},{24,8},{1,17},{9,25},{17,1},{25,9},{2,18},{10... | collective-permute-start | bytes 49160 | tf_op jit(solution)/shard_map/ppermute | solution.py:354
where the time goes:
time: 76.7 us; the launch traced here: 76.5 us
  starting transfers between devices  39 us (51%)
  waiting for transfers between devices  23.8 us (31%)
  Pallas kernels  12.8 us (17%)
  between operations  0.8 us (1%)
    ppermute x6, starting transfers between devices, along_z(): return lax.ppermute(x, 'tgt', pairs)  10.7 us
    ppermute x4, starting transfers between devices, reduce_lists(): from_z = lax.ppermute(fwd, 'tgt', pairs)  9.04 us
    ppermute x9, starting transfers between devices, swap(): return lax.ppermute(x, 'tgt', partner)  8.62 us
    ppermute x4, waiting for transfers between devices, reduce_lists(): from_z = lax.ppermute(fwd, 'tgt', pairs)  7.81 us
    ppermute x4, waiting for transfers between devices, reduce_lists(): from_src = lax.ppermute(bwd, 'src', pairs)  6.36 us
    ppermute x4, starting transfers between devices, reduce_lists(): from_src = lax.ppermute(bwd, 'src', pairs)  6.03 us
    ppermute x3, waiting for transfers between devices, along_src(): return lax.ppermute(x, both, pairs)  5.65 us
    pallas_call x1, Pallas kernels, compute(): pl.pallas_call(functools.partial(score_kernel, depth, [at for _, at in la...  4.97 us
  transfers between devices with their start and end apart: 26, of which 12 were waited for; matrix products, arithmetic and copies ran while one was open for 0% of the time, Pallas kernels for 4%

commit v1 on v0

--- a/solution.py
+++ b/solution.py
@@ -187,7 +187,7 @@
 
 
 def score_kernel(depth, places, mine_ref, theirs_ref, tgt_buf, _, column, lane, part,
-                 src_buf, sim, fwd, bwd, one, two, state, src_sem):
+                 src_buf, sim, fwd, state, one, two, src_sem):
     t = lax.axis_index("tgt")
     core, z = t % 2, t // 2
     sources, targets = src_buf.shape[1], tgt_buf.shape[1]
@@ -209,9 +209,6 @@
         else:
             out[...] = product(tgt_buf[:, cols], src_buf[:, pl.ds(g * GROUP, GROUP)])
 
-    def write_rows(k, c, row):
-        bwd[k, pl.ds(c, 1), :] = row
-
     dot(*blocks[0], one)
     for i, (g, r) in enumerate(blocks):
         now, later = (one, two) if i % 2 == 0 else (two, one)
@@ -236,16 +233,26 @@
                     fwd[pl.ds(k * ns + g * 4 + b, 1), :] = best[k][0:1, :]
     if sources == GROUP:
         each(lambda c: c.wait())
-    finish_rows(targets, write_rows, state)
-
-
-def margin_kernel(sim, fwd_mine, fwd_other, bwd_all, fwd, bwd, column, lane, state):
+
+
+def finish_kernel(state, bwd):
+    def write(k, c, row):
+        bwd[k, pl.ds(c, 1), :] = row
+
+    finish_rows(state.shape[1], write, state)
+
+
+def column_kernel(mine, rec, column):
+    b = merge4(split_list(mine), split_list(rec))
+    b = 0.5 * (0.25 * (b[0] + b[1] + b[2] + b[3]))
+    for c in range(column.shape[0] // LANES):
+        column[pl.ds(c * LANES, LANES), :] = column_of(b[c : c + 1, :])
+
+
+def margin_kernel(sim, fwd_mine, fwd_other, column, fwd, state, lane):
     targets, sources = sim.shape
     f = merge4(split_list(fwd_mine), split_list(fwd_other))
     f = 0.5 * (0.25 * (f[0] + f[1] + f[2] + f[3]))
-    b = 0.5 * (0.25 * (bwd_all[0] + bwd_all[1] + bwd_all[2] + bwd_all[3]))
-    for c in range(targets // LANES):
-        column[pl.ds(c * LANES, LANES), :] = column_of(b[c : c + 1, :])
     for c in range(sources // LANES):
         lane[:, pl.ds(c * LANES, LANES)] = jnp.broadcast_to(f[c : c + 1, :], (8, LANES))
     rows = math.gcd(targets, 256)
@@ -253,9 +260,6 @@
     def write(k, c, row):
         fwd[pl.ds(k * (sources // LANES) + c, 1), :] = row
 
-    def write_rows(k, c, row):
-        bwd[k, pl.ds(c, 1), :] = row
-
     for g in range(sources // GROUP):
 
         def body(q, lists, g=g):
@@ -268,7 +272,6 @@
             return sweep_block(load, base, rows, g == 0, lists, state)
 
         loop_lists(targets // rows, body, write, g)
-    finish_rows(targets, write_rows, state)
 
 
 def split_list(ref):
@@ -344,24 +347,33 @@
             merge_kernel, out_shape=f32(*mine.shape), in_specs=[VMEM] * 2, out_specs=VMEM,
             compiler_params=params(1), name="merge")(mine, rec)
 
-    def reduce_lists(fwd, bwd):
+    def reduce_lists(fwd, state, columns):
+        targets = state.shape[1]
         for step in range(max(src_bits, z_bits)):
             if step < z_bits:
                 pairs = [(t, t ^ (2 << step)) for t in range(n_tgt)]
                 from_z = lax.ppermute(fwd, "tgt", pairs)
+            if step == 0:
+                bwd = pl.pallas_call(
+                    finish_kernel, out_shape=f32(TOP, targets // LANES, LANES), in_specs=[VMEM], out_specs=VMEM,
+                    compiler_params=params(1), name="finish")(state)
             if step < src_bits:
                 pairs = [(s, s ^ (1 << step)) for s in range(n_src)]
                 from_src = lax.ppermute(bwd, "src", pairs)
             if step < z_bits:
                 fwd = merged(fwd, from_z)
-            if step < src_bits:
+            if step + 1 == src_bits and columns:
+                bwd = pl.pallas_call(
+                    column_kernel, out_shape=f32(targets, LANES), in_specs=[VMEM] * 2, out_specs=VMEM,
+                    compiler_params=params(1), name="column")(bwd, from_src)
+            elif step < src_bits:
                 bwd = merged(bwd, from_src)
         return fwd, swap(fwd), bwd
 
     def compute(src_codes, src_scale, tgt_codes, tgt_scale):
         sources, targets = src_codes.shape[1], tgt_codes.shape[1]
         total = src_codes.shape[0] * n_tgt
-        ns, nt = sources // LANES, targets // LANES
+        ns = sources // LANES
         scale_s, scale_t = src_scale.reshape(-1, LANES), tgt_scale.reshape(-1, LANES)
 
         u, v = src_codes, swap(src_codes)
@@ -401,37 +413,32 @@
             [(in_hbm(tgt_codes), (0, 0))] + held[1:-1], [(in_hbm(src_codes), own[0][1]), own[1]] + passed[:-6],
             (in_hbm(scale_s), in_hbm(scale_t)), True)
         tgt_block, src_block, part = prep(held[-1:], passed[-6:], (tgt_block, src_block), False)
-        block = min(512, targets // 2)
-        _, sim, fwd, bwd = pl.pallas_call(
+        block = min(256, targets // 2)
+        _, sim, fwd, state = pl.pallas_call(
             functools.partial(score_kernel, depth, [at for _, at in late]),
             out_shape=(jax.ShapeDtypeStruct((total, sources), src_codes.dtype),
-                       f32(targets, sources), f32(TOP * ns, LANES), f32(TOP, nt, LANES)),
+                       f32(targets, sources), f32(TOP * ns, LANES), f32(TOP, targets, LANES)),
             in_specs=[VMEM] * 7, out_specs=(VMEM,) * 4,
             input_output_aliases={3: 0},
             scratch_shapes=[
                 pltpu.VMEM((block, GROUP), jnp.float32),
                 pltpu.VMEM((block, GROUP), jnp.float32),
-                pltpu.VMEM((TOP, targets, LANES), jnp.float32),
                 pltpu.SemaphoreType.DMA((2,)),
             ],
             compiler_params=params(8), cost_estimate=cost(2 * total * sources * targets, 4 * sources * targets),
             name="score")(*[x for x, _ in late], tgt_block, src_block, column, lane, part)
 
-        fwd, bwd = pl.pallas_call(
+        fwd, state = pl.pallas_call(
             margin_kernel,
-            out_shape=(f32(TOP * ns, LANES), f32(TOP, nt, LANES)),
+            out_shape=(f32(TOP * ns, LANES), f32(TOP, targets, LANES)),
             in_specs=[VMEM] * 4, out_specs=(VMEM,) * 2,
-            scratch_shapes=[
-                pltpu.VMEM((targets, LANES), jnp.float32),
-                pltpu.VMEM((8, sources), jnp.float32),
-                pltpu.VMEM((TOP, targets, LANES), jnp.float32),
-            ],
-            compiler_params=params(8), cost_estimate=cost(30 * sources * targets, 4 * sources * targets),
-            name="margin")(sim, *reduce_lists(fwd, bwd))
+            scratch_shapes=[pltpu.VMEM((8, sources), jnp.float32)],
+            compiler_params=params(4), cost_estimate=cost(30 * sources * targets, 4 * sources * targets),
+            name="margin")(sim, *reduce_lists(fwd, state, True))
         return pl.pallas_call(
             final_kernel, out_shape=(f32(TOP, sources), f32(TOP, targets)),
             in_specs=[VMEM] * 3, out_specs=(VMEM,) * 2, compiler_params=params(1),
-            name="final")(*reduce_lists(fwd, bwd))
+            name="final")(*reduce_lists(fwd, state, False))
 
     placed = (P("tgt", "src"), P("src"), P("src", "tgt"), P("tgt"))
     return jax.shard_map(

time: 76.7 us -> 76.9 us (level)
    ppermute x4, starting transfers between devices: 9.04 us -> 8.13 us  [reduce_lists(): from_z = lax.ppermute(fwd, 'tgt', pairs)]
    pallas_call x1 -> x4, Pallas kernels: 3.78 us -> 4.52 us  [the longest x1 3.07 us: compute(): pl.pallas_call(margin_kernel, out_shape=(f32(TOP * ns, LANES), f32(TOP, t...]
  transfers between devices with their start and end apart: 26 -> 26, of which waited for: 12 -> 10; matrix products, arithmetic and copies ran while one was open for 0% -> 0% of each run, Pallas kernels for 4% -> 6%
where the time goes in v1:
time: 76.9 us; the launch traced here: 76.7 us
  starting transfers between devices  38.3 us (50%)
  waiting for transfers between devices  24.2 us (31%)
  Pallas kernels  13.4 us (17%)
  between operations  0.84 us (1%)
    ppermute x6, starting transfers between devices, along_z(): return lax.ppermute(x, 'tgt', pairs)  10.7 us
    ppermute x9, starting transfers between devices, swap(): return lax.ppermute(x, 'tgt', partner)  8.62 us
    ppermute x4, starting transfers between devices, reduce_lists(): from_z = lax.ppermute(fwd, 'tgt', pairs)  8.13 us
    ppermute x4, waiting for transfers between devices, reduce_lists(): from_z = lax.ppermute(fwd, 'tgt', pairs)  7.94 us
    ppermute x4, waiting for transfers between devices, reduce_lists(): from_src = lax.ppermute(bwd, 'src', pairs)  6.6 us
    ppermute x4, starting transfers between devices, reduce_lists(): from_src = lax.ppermute(bwd, 'src', pairs)  6.21 us
    ppermute x3, waiting for transfers between devices, along_src(): return lax.ppermute(x, both, pairs)  5.65 us
    pallas_call x1, Pallas kernels, compute(): pl.pallas_call(functools.partial(score_kernel, depth, [at for _, at in la...  4.78 us
  transfers between devices with their start and end apart: 26, of which 10 were waited for; matrix products, arithmetic and copies ran while one was open for 0% of the time, Pallas kernels for 6%

profile of v1, /device:TPU:0, one launch (start us, length us, event | category | flops | bytes accessed | tf_op | source)
XLA Modules:
  0.0 76.7 jit_solution(12811957592041954569)
XLA Ops:
  1.2 4.5 %collective-permute-start.7 = (bf16[128,1536]{1,0:T(8,128)(2,1)}, bf16[128,1536]{1,0:T(8,128)(2,1)S(1)}, u32[]{:S(2)}, u32[]{:S(2)}) collective-permute-start(bf16[128,1536]{1,0:T(8,128)(2,1)} %refs_3_.1), channel_id=1, source_target_pairs={{0,2},{2,4},{3,1},{4,6},{5,3},{7,5},{8,10},{10,12},{11,9},{12,14},... | collective-permute-start | bytes 1179656 | tf_op jit(solution)/shard_map/ppermute | solution.py:336
  5.7 3.5 %collective-permute-start.1 = (bf16[128,1536]{1,0:T(8,128)(2,1)S(1)}, bf16[128,1536]{1,0:T(8,128)(2,1)S(1)}, u32[]{:S(2)}, u32[]{:S(2)}) collective-permute-start(bf16[128,1536]{1,0:T(8,128)(2,1)S(1)} %collective-permute-done.refs_4_), channel_id=1, source_target_pairs={{0,2},{2,4},{3,1},{4,6},{5,3},{7,5},{8,10},{10,12},{11,9},{12,14},... | collective-permute-start | bytes 1179656 | tf_op jit(solution)/shard_map/ppermute | solution.py:336
  9.2 1.6 %collective-permute-start.5 = (bf16[256,1024]{1,0:T(8,128)(2,1)}, bf16[256,1024]{1,0:T(8,128)(2,1)S(1)}, u32[]{:S(2)}, u32[]{:S(2)}) collective-permute-start(bf16[256,1024]{1,0:T(8,128)(2,1)} %refs_0_.1), channel_id=1, source_target_pairs={{0,8},{1,17},{2,10},{3,19},{4,12},{5,21},{6,14},{7,23},{8,0},{9,25... | collective-permute-start | bytes 1572872 | tf_op jit(solution)/shard_map/ppermute | solution.py:343
  11.3 0.7 collective-permute-start.8
  11.9 3.4 %collective-permute-done.1.refs_7_ = bf16[128,1536]{1,0:T(8,128)(2,1)S(1)} collective-permute-done((bf16[128,1536]{1,0:T(8,128)(2,1)S(1)}, bf16[128,1536]{1,0:T(8,128)(2,1)S(1)}, u32[]{:S(2)}, u32[]{:S(2)}) %collective-permute-start.1) | collective-permute-done | bytes 393248 | tf_op jit(solution)/shard_map/ppermute | solution.py:336
  15.4 0.7 collective-permute-start.2
  16.1 1.6 %collective-permute-start.13 = (bf16[256,1024]{1,0:T(8,128)(2,1)}, bf16[256,1024]{1,0:T(8,128)(2,1)S(1)}, u32[]{:S(2)}, u32[]{:S(2)}) collective-permute-start(bf16[256,1024]{1,0:T(8,128)(2,1)} %refs_0_.1), channel_id=1, source_target_pairs={{0,16},{1,9},{2,18},{3,11},{4,20},{5,13},{6,22},{7,15},{8,24},{9,1... | collective-permute-start | bytes 1572872 | tf_op jit(solution)/shard_map/ppermute | solution.py:343
  17.6 0.8 %collective-permute-start.14 = (bf16[128,1536]{1,0:T(8,128)(2,1)S(1)}, bf16[128,1536]{1,0:T(8,128)(2,1)S(1)}, u32[]{:S(2)}, u32[]{:S(2)}) collective-permute-start(bf16[128,1536]{1,0:T(8,128)(2,1)S(1)} %collective-permute-done.7.refs_5_), channel_id=1, source_target_pairs={{0,1},{1,0},{2,3},{3,2},{4,5},{5,4},{6,7},{7,6},{8,9},{9,8},{10,11... | collective-permute-start | bytes 1179656 | tf_op jit(solution)/shard_map/ppermute | solution.py:326
  18.7 0.7 collective-permute-start.11
  19.4 0.7 collective-permute-start.3
  20.1 5.5 %collective-permute-done.13.refs_2_ = bf16[256,1024]{1,0:T(8,128)(2,1)S(1)} collective-permute-done((bf16[256,1024]{1,0:T(8,128)(2,1)}, bf16[256,1024]{1,0:T(8,128)(2,1)S(1)}, u32[]{:S(2)}, u32[]{:S(2)}) %collective-permute-start.13) | collective-permute-done | bytes 524320 | tf_op jit(solution)/shard_map/ppermute | solution.py:343
  25.5 1.5 %collective-permute-start.6 = (bf16[256,1024]{1,0:T(8,128)(2,1)S(1)}, bf16[256,1024]{1,0:T(8,128)(2,1)S(1)}, u32[]{:S(2)}, u32[]{:S(2)}) collective-permute-start(bf16[256,1024]{1,0:T(8,128)(2,1)S(1)} %collective-permute-done.5.refs_1_), channel_id=1, source_target_pairs={{0,16},{1,9},{2,18},{3,11},{4,20},{5,13},{6,22},{7,15},{8,24},{9,1... | collective-permute-start | bytes 1572872 | tf_op jit(solution)/shard_map/ppermute | solution.py:343
  27.6 2.4 %collective-permute-start.12 = (bf16[128,1536]{1,0:T(8,128)(2,1)S(1)}, bf16[128,1536]{1,0:T(8,128)(2,1)S(1)}, u32[]{:S(2)}, u32[]{:S(2)}) collective-permute-start(bf16[128,1536]{1,0:T(8,128)(2,1)S(1)} %collective-permute-done.11.refs_5_), channel_id=1, source_target_pairs={{0,1},{1,0},{2,3},{3,2},{4,5},{5,4},{6,7},{7,6},{8,9},{9,8},{10,11... | collective-permute-start | bytes 1179656 | tf_op jit(solution)/shard_map/ppermute | solution.py:326
  29.9 4.2 %collective-permute-start.4 = (bf16[128,1536]{1,0:T(8,128)(2,1)S(1)}, bf16[128,1536]{1,0:T(8,128)(2,1)S(1)}, u32[]{:S(2)}, u32[]{:S(2)}) collective-permute-start(bf16[128,1536]{1,0:T(8,128)(2,1)S(1)} %collective-permute-done.3.mine_ref), channel_id=1, source_target_pairs={{0,1},{1,0},{2,3},{3,2},{4,5},{5,4},{6,7},{7,6},{8,9},{9,8},{10,11... | collective-permute-start | bytes 1179656 | tf_op jit(solution)/shard_map/ppermute | solution.py:326
  34.1 1.3 %shard_map.59 = (bf16[1024,1024]{1,0:T(8,128)(2,1)S(1)}, bf16[1024,1536]{1,0:T(8,128)(2,1)S(1)}, f32[1024,128]{1,0:T(8,128)S(1)}, f32[8,1536]{1,0:T(8,128)S(1)}) custom-call(bf16[256,1024]{1,0:T(8,128)(2,1)} %refs_0_.1, bf16[256,1024]{1,0:T(8,128)(2,1)S(1)} %collective-permute-done.5.refs_1_, bf16[256,1024]{1,0:T(8,128)(2,1)S(1)} %collective-permute-done.13.refs_2_, ...), custom_call_target="tpu_custom_call" | custom-call | bytes 4194304 | tf_op jit(solution)/shard_map/pallas_call | solution.py:405
  35.5 2.1 %shard_map.60 = (bf16[1024,1024]{1,0:T(8,128)(2,1)S(1)}, bf16[1024,1536]{1,0:T(8,128)(2,1)S(1)}, f32[1024,512]{1,0:T(8,128)S(1)}) custom-call(bf16[256,1024]{1,0:T(8,128)(2,1)S(1)} %collective-permute-done.6.refs_0_, bf16[128,1536]{1,0:T(8,128)(2,1)S(1)} %collective-permute-done.8.refs_1_, ...), custom_call_target="tpu_custom_call", output_to_operand_aliasing={{0}: (7, {}), {1}: (8, {})} | custom-call | bytes 4194304 | tf_op jit(solution)/shard_map/pallas_call | solution.py:405
  37.6 4.8 %score.1 = (bf16[1024,1536]{1,0:T(8,128)(2,1)S(1)}, f32[1024,1536]{1,0:T(8,128)S(1)}, f32[48,128]{1,0:T(8,128)S(1)}, f32[4,1024,128]{2,1,0:T(8,128)S(1)}) custom-call(bf16[128,1536]{1,0:T(8,128)(2,1)S(1)} %collective-permute-done.3.mine_ref, bf16[128,1536]{1,0:T(8,128)(2,1)S(1)} %collective-permute-done.4.theirs_ref, ...), custom_call_target="tpu_custom_call", output_to_operand_aliasing={{0}: (3, {})} | custom-call | flops 3221225472 | bytes 6291456 | tf_op jit(solution)/shard_map/score/pallas_call | solution.py:417
  42.3 4.2 %collective-permute-start.16 = (f32[48,128]{1,0:T(8,128)S(1)}, f32[48,128]{1,0:T(8,128)S(1)}, u32[]{:S(2)}, u32[]{:S(2)}) collective-permute-start(f32[48,128]{1,0:T(8,128)S(1)} %get-tuple-element.22.mine), channel_id=1, source_target_pairs={{0,2},{1,3},{2,0},{3,1},{4,6},{5,7},{6,4},{7,5},{8,10},{9,11},{10,... | collective-permute-start | bytes 73736 | tf_op jit(solution)/shard_map/ppermute | solution.py:355
  46.5 1.8 %collective-permute-done.16.rec = f32[48,128]{1,0:T(8,128)S(1)} collective-permute-done((f32[48,128]{1,0:T(8,128)S(1)}, f32[48,128]{1,0:T(8,128)S(1)}, u32[]{:S(2)}, u32[]{:S(2)}) %collective-permute-start.16) | collective-permute-done | bytes 24608 | tf_op jit(solution)/shard_map/ppermute | solution.py:355
  48.3 3.4 %collective-permute-start.17 = (f32[48,128]{1,0:T(8,128)S(1)}, f32[48,128]{1,0:T(8,128)S(1)}, u32[]{:S(2)}, u32[]{:S(2)}) collective-permute-start(f32[48,128]{1,0:T(8,128)S(1)} %merge.7.mine), channel_id=1, source_target_pairs={{0,4},{1,5},{2,6},{3,7},{4,0},{5,1},{6,2},{7,3},{8,12},{9,13},{10,... | collective-permute-start | bytes 73736 | tf_op jit(solution)/shard_map/ppermute | solution.py:355
  51.7 0.6 finish.2.mine
  52.3 1.6 %collective-permute-start.19 = (f32[4,8,128]{2,1,0:T(8,128)S(1)}, f32[4,8,128]{2,1,0:T(8,128)S(1)}, u32[]{:S(2)}, u32[]{:S(2)}) collective-permute-start(f32[4,8,128]{2,1,0:T(8,128)S(1)} %finish.2.mine), channel_id=1, source_target_pairs={{0,8},{8,0},{16,24},{24,16},{1,9},{9,1},{17,25},{25,17},{2,10},{10... | collective-permute-start | bytes 49160 | tf_op jit(solution)/shard_map/ppermute | solution.py:362
  54.0 2.2 %collective-permute-done.19.rec = f32[4,8,128]{2,1,0:T(8,128)S(1)} collective-permute-done((f32[4,8,128]{2,1,0:T(8,128)S(1)}, f32[4,8,128]{2,1,0:T(8,128)S(1)}, u32[]{:S(2)}, u32[]{:S(2)}) %collective-permute-start.19) | collective-permute-done | bytes 16416 | tf_op jit(solution)/shard_map/ppermute | solution.py:362
  56.2 1.5 %collective-permute-start.20 = (f32[4,8,128]{2,1,0:T(8,128)S(1)}, f32[4,8,128]{2,1,0:T(8,128)S(1)}, u32[]{:S(2)}, u32[]{:S(2)}) collective-permute-start(f32[4,8,128]{2,1,0:T(8,128)S(1)} %merge.9.mine), channel_id=1, source_target_pairs={{0,16},{8,24},{16,0},{24,8},{1,17},{9,25},{17,1},{25,9},{2,18},{10... | collective-permute-start | bytes 49160 | tf_op jit(solution)/shard_map/ppermute | solution.py:362
  57.7 2.2 %collective-permute-done.20.rec = f32[4,8,128]{2,1,0:T(8,128)S(1)} collective-permute-done((f32[4,8,128]{2,1,0:T(8,128)S(1)}, f32[4,8,128]{2,1,0:T(8,128)S(1)}, u32[]{:S(2)}, u32[]{:S(2)}) %collective-permute-start.20) | collective-permute-done | bytes 16416 | tf_op jit(solution)/shard_map/ppermute | solution.py:362
  60.1 3.1 %margin.1 = (f32[48,128]{1,0:T(8,128)S(1)}, f32[4,1024,128]{2,1,0:T(8,128)S(1)}) custom-call(f32[1024,1536]{1,0:T(8,128)S(1)} %get-tuple-element.21.sim, f32[48,128]{1,0:T(8,128)S(1)} %merge.8.fwd_mine, f32[48,128]{1,0:T(8,128)S(1)} %collective-permute-done.18.fwd_other, f32[1024,128]{1,0:T(8,128)S(1)} %column.1), custom_call_target="tpu_custom_call" | custom-call | flops 47185920 | bytes 6291456 | tf_op jit(solution)/shard_map/margin/pallas_call | solution.py:431
  63.4 3.8 %collective-permute-done.21.rec = f32[48,128]{1,0:T(8,128)S(1)} collective-permute-done((f32[48,128]{1,0:T(8,128)S(1)}, f32[48,128]{1,0:T(8,128)S(1)}, u32[]{:S(2)}, u32[]{:S(2)}) %collective-permute-start.21) | collective-permute-done | bytes 24608 | tf_op jit(solution)/shard_map/ppermute | solution.py:355
  68.2 1.6 %collective-permute-start.24 = (f32[4,8,128]{2,1,0:T(8,128)S(1)}, f32[4,8,128]{2,1,0:T(8,128)S(1)}, u32[]{:S(2)}, u32[]{:S(2)}) collective-permute-start(f32[4,8,128]{2,1,0:T(8,128)S(1)} %finish.3.mine), channel_id=1, source_target_pairs={{0,8},{8,0},{16,24},{24,16},{1,9},{9,1},{17,25},{25,17},{2,10},{10... | collective-permute-start | bytes 49160 | tf_op jit(solution)/shard_map/ppermute | solution.py:362
  69.8 2.3 %collective-permute-done.22.rec = f32[48,128]{1,0:T(8,128)S(1)} collective-permute-done((f32[48,128]{1,0:T(8,128)S(1)}, f32[48,128]{1,0:T(8,128)S(1)}, u32[]{:S(2)}, u32[]{:S(2)}) %collective-permute-start.22) | collective-permute-done | bytes 24608 | tf_op jit(solution)/shard_map/ppermute | solution.py:355
  72.2 1.6 %collective-permute-start.25 = (f32[4,8,128]{2,1,0:T(8,128)S(1)}, f32[4,8,128]{2,1,0:T(8,128)S(1)}, u32[]{:S(2)}, u32[]{:S(2)}) collective-permute-start(f32[4,8,128]{2,1,0:T(8,128)S(1)} %merge.12.mine), channel_id=1, source_target_pairs={{0,16},{8,24},{16,0},{24,8},{1,17},{9,25},{17,1},{25,9},{2,18},{10... | collective-permute-start | bytes 49160 | tf_op jit(solution)/shard_map/ppermute | solution.py:362
  73.8 2.2 %collective-permute-done.25.rec = f32[4,8,128]{2,1,0:T(8,128)S(1)} collective-permute-done((f32[4,8,128]{2,1,0:T(8,128)S(1)}, f32[4,8,128]{2,1,0:T(8,128)S(1)}, u32[]{:S(2)}, u32[]{:S(2)}) %collective-permute-start.25) | collective-permute-done | bytes 16416 | tf_op jit(solution)/shard_map/ppermute | solution.py:362
  76.0 0.6 final.1
  (35 shorter events, 3.4 us)
Async XLA Ops:
  0.6 5.1 %collective-permute-start = (bf16[128,1536]{1,0:T(8,128)(2,1)}, bf16[128,1536]{1,0:T(8,128)(2,1)S(1)}, u32[]{:S(2)}, u32[]{:S(2)}) collective-permute-start(bf16[128,1536]{1,0:T(8,128)(2,1)} %refs_3_.1), channel_id=1, source_target_pairs={{0,1},{1,0},{2,3},{3,2},{4,5},{5,4},{6,7},{7,6},{8,9},{9,8},{10,11... | collective-permute-start | bytes 1179656 | tf_op jit(solution)/shard_map/ppermute | solution.py:326
  1.2 10.1 %collective-permute-start.7 = (bf16[128,1536]{1,0:T(8,128)(2,1)}, bf16[128,1536]{1,0:T(8,128)(2,1)S(1)}, u32[]{:S(2)}, u32[]{:S(2)}) collective-permute-start(bf16[128,1536]{1,0:T(8,128)(2,1)} %refs_3_.1), channel_id=1, source_target_pairs={{0,2},{2,4},{3,1},{4,6},{5,3},{7,5},{8,10},{10,12},{11,9},{12,14},... | collective-permute-start | bytes 1179656 | tf_op jit(solution)/shard_map/ppermute | solution.py:336
  5.7 9.7 %collective-permute-start.1 = (bf16[128,1536]{1,0:T(8,128)(2,1)S(1)}, bf16[128,1536]{1,0:T(8,128)(2,1)S(1)}, u32[]{:S(2)}, u32[]{:S(2)}) collective-permute-start(bf16[128,1536]{1,0:T(8,128)(2,1)S(1)} %collective-permute-done.refs_4_), channel_id=1, source_target_pairs={{0,2},{2,4},{3,1},{4,6},{5,3},{7,5},{8,10},{10,12},{11,9},{12,14},... | collective-permute-start | bytes 1179656 | tf_op jit(solution)/shard_map/ppermute | solution.py:336
  9.2 9.5 %collective-permute-start.5 = (bf16[256,1024]{1,0:T(8,128)(2,1)}, bf16[256,1024]{1,0:T(8,128)(2,1)S(1)}, u32[]{:S(2)}, u32[]{:S(2)}) collective-permute-start(bf16[256,1024]{1,0:T(8,128)(2,1)} %refs_0_.1), channel_id=1, source_target_pairs={{0,8},{1,17},{2,10},{3,19},{4,12},{5,21},{6,14},{7,23},{8,0},{9,25... | collective-permute-start | bytes 1572872 | tf_op jit(solution)/shard_map/ppermute | solution.py:343
  11.3 7.4 %collective-permute-start.8 = (bf16[128,1536]{1,0:T(8,128)(2,1)S(1)}, bf16[128,1536]{1,0:T(8,128)(2,1)S(1)}, u32[]{:S(2)}, u32[]{:S(2)}) collective-permute-start(bf16[128,1536]{1,0:T(8,128)(2,1)S(1)} %collective-permute-done.7.refs_5_), channel_id=1, source_target_pairs={{2,4},{3,1},{4,6},{5,3},{10,12},{11,9},{12,14},{13,11},{18,20},{19... | collective-permute-start | bytes 1179656 | tf_op jit(solution)/shard_map/ppermute | solution.py:336
  15.4 4.0 %collective-permute-start.2 = (bf16[128,1536]{1,0:T(8,128)(2,1)S(1)}, bf16[128,1536]{1,0:T(8,128)(2,1)S(1)}, u32[]{:S(2)}, u32[]{:S(2)}) collective-permute-start(bf16[128,1536]{1,0:T(8,128)(2,1)S(1)} %collective-permute-done.1.refs_7_), channel_id=1, source_target_pairs={{2,4},{3,1},{4,6},{5,3},{10,12},{11,9},{12,14},{13,11},{18,20},{19... | collective-permute-start | bytes 1179656 | tf_op jit(solution)/shard_map/ppermute | solution.py:336
  16.1 9.5 %collective-permute-start.13 = (bf16[256,1024]{1,0:T(8,128)(2,1)}, bf16[256,1024]{1,0:T(8,128)(2,1)S(1)}, u32[]{:S(2)}, u32[]{:S(2)}) collective-permute-start(bf16[256,1024]{1,0:T(8,128)(2,1)} %refs_0_.1), channel_id=1, source_target_pairs={{0,16},{1,9},{2,18},{3,11},{4,20},{5,13},{6,22},{7,15},{8,24},{9,1... | collective-permute-start | bytes 1572872 | tf_op jit(solution)/shard_map/ppermute | solution.py:343
  17.6 9.4 %collective-permute-start.14 = (bf16[128,1536]{1,0:T(8,128)(2,1)S(1)}, bf16[128,1536]{1,0:T(8,128)(2,1)S(1)}, u32[]{:S(2)}, u32[]{:S(2)}) collective-permute-start(bf16[128,1536]{1,0:T(8,128)(2,1)S(1)} %collective-permute-done.7.refs_5_), channel_id=1, source_target_pairs={{0,1},{1,0},{2,3},{3,2},{4,5},{5,4},{6,7},{7,6},{8,9},{9,8},{10,11... | collective-permute-start | bytes 1179656 | tf_op jit(solution)/shard_map/ppermute | solution.py:326
  18.7 8.6 %collective-permute-start.15 = (bf16[128,1536]{1,0:T(8,128)(2,1)S(1)}, bf16[128,1536]{1,0:T(8,128)(2,1)S(1)}, u32[]{:S(2)}, u32[]{:S(2)}) collective-permute-start(bf16[128,1536]{1,0:T(8,128)(2,1)S(1)} %collective-permute-done.1.refs_7_), channel_id=1, source_target_pairs={{0,1},{1,0},{2,3},{3,2},{4,5},{5,4},{6,7},{7,6},{8,9},{9,8},{10,11... | collective-permute-start | bytes 1179656 | tf_op jit(solution)/shard_map/ppermute | solution.py:326
  18.7 8.9 %collective-permute-start.11 = (bf16[128,1536]{1,0:T(8,128)(2,1)S(1)}, bf16[128,1536]{1,0:T(8,128)(2,1)S(1)}, u32[]{:S(2)}, u32[]{:S(2)}) collective-permute-start(bf16[128,1536]{1,0:T(8,128)(2,1)S(1)} %collective-permute-done.8.refs_1_), channel_id=1, source_target_pairs={{3,1},{4,6},{11,9},{12,14},{19,17},{20,22},{27,25},{28,30}} | collective-permute-start | bytes 1179656 | tf_op jit(solution)/shard_map/ppermute | solution.py:336
  19.4 10.6 %collective-permute-start.3 = (bf16[128,1536]{1,0:T(8,128)(2,1)S(1)}, bf16[128,1536]{1,0:T(8,128)(2,1)S(1)}, u32[]{:S(2)}, u32[]{:S(2)}) collective-permute-start(bf16[128,1536]{1,0:T(8,128)(2,1)S(1)} %collective-permute-done.2.refs_3_), channel_id=1, source_target_pairs={{3,1},{4,6},{11,9},{12,14},{19,17},{20,22},{27,25},{28,30}} | collective-permute-start | bytes 1179656 | tf_op jit(solution)/shard_map/ppermute | solution.py:336
  25.5 9.9 %collective-permute-start.6 = (bf16[256,1024]{1,0:T(8,128)(2,1)S(1)}, bf16[256,1024]{1,0:T(8,128)(2,1)S(1)}, u32[]{:S(2)}, u32[]{:S(2)}) collective-permute-start(bf16[256,1024]{1,0:T(8,128)(2,1)S(1)} %collective-permute-done.5.refs_1_), channel_id=1, source_target_pairs={{0,16},{1,9},{2,18},{3,11},{4,20},{5,13},{6,22},{7,15},{8,24},{9,1... | collective-permute-start | bytes 1572872 | tf_op jit(solution)/shard_map/ppermute | solution.py:343
  27.0 8.4 %collective-permute-start.9 = (bf16[128,1536]{1,0:T(8,128)(2,1)S(1)}, bf16[128,1536]{1,0:T(8,128)(2,1)S(1)}, u32[]{:S(2)}, u32[]{:S(2)}) collective-permute-start(bf16[128,1536]{1,0:T(8,128)(2,1)S(1)} %collective-permute-done.8.refs_1_), channel_id=1, source_target_pairs={{0,1},{1,0},{2,3},{3,2},{4,5},{5,4},{6,7},{7,6},{8,9},{9,8},{10,11... | collective-permute-start | bytes 1179656 | tf_op jit(solution)/shard_map/ppermute | solution.py:326
  27.3 8.2 %collective-permute-start.10 = (bf16[128,1536]{1,0:T(8,128)(2,1)S(1)}, bf16[128,1536]{1,0:T(8,128)(2,1)S(1)}, u32[]{:S(2)}, u32[]{:S(2)}) collective-permute-start(bf16[128,1536]{1,0:T(8,128)(2,1)S(1)} %collective-permute-done.2.refs_3_), channel_id=1, source_target_pairs={{0,1},{1,0},{2,3},{3,2},{4,5},{5,4},{6,7},{7,6},{8,9},{9,8},{10,11... | collective-permute-start | bytes 1179656 | tf_op jit(solution)/shard_map/ppermute | solution.py:326
  27.6 7.9 %collective-permute-start.12 = (bf16[128,1536]{1,0:T(8,128)(2,1)S(1)}, bf16[128,1536]{1,0:T(8,128)(2,1)S(1)}, u32[]{:S(2)}, u32[]{:S(2)}) collective-permute-start(bf16[128,1536]{1,0:T(8,128)(2,1)S(1)} %collective-permute-done.11.refs_5_), channel_id=1, source_target_pairs={{0,1},{1,0},{2,3},{3,2},{4,5},{5,4},{6,7},{7,6},{8,9},{9,8},{10,11... | collective-permute-start | bytes 1179656 | tf_op jit(solution)/shard_map/ppermute | solution.py:326
  29.9 7.6 %collective-permute-start.4 = (bf16[128,1536]{1,0:T(8,128)(2,1)S(1)}, bf16[128,1536]{1,0:T(8,128)(2,1)S(1)}, u32[]{:S(2)}, u32[]{:S(2)}) collective-permute-start(bf16[128,1536]{1,0:T(8,128)(2,1)S(1)} %collective-permute-done.3.mine_ref), channel_id=1, source_target_pairs={{0,1},{1,0},{2,3},{3,2},{4,5},{5,4},{6,7},{7,6},{8,9},{9,8},{10,11... | collective-permute-start | bytes 1179656 | tf_op jit(solution)/shard_map/ppermute | solution.py:326
  42.3 6.0 %collective-permute-start.16 = (f32[48,128]{1,0:T(8,128)S(1)}, f32[48,128]{1,0:T(8,128)S(1)}, u32[]{:S(2)}, u32[]{:S(2)}) collective-permute-start(f32[48,128]{1,0:T(8,128)S(1)} %get-tuple-element.22.mine), channel_id=1, source_target_pairs={{0,2},{1,3},{2,0},{3,1},{4,6},{5,7},{6,4},{7,5},{8,10},{9,11},{10,... | collective-permute-start | bytes 73736 | tf_op jit(solution)/shard_map/ppermute | solution.py:355
  48.3 5.6 %collective-permute-start.17 = (f32[48,128]{1,0:T(8,128)S(1)}, f32[48,128]{1,0:T(8,128)S(1)}, u32[]{:S(2)}, u32[]{:S(2)}) collective-permute-start(f32[48,128]{1,0:T(8,128)S(1)} %merge.7.mine), channel_id=1, source_target_pairs={{0,4},{1,5},{2,6},{3,7},{4,0},{5,1},{6,2},{7,3},{8,12},{9,13},{10,... | collective-permute-start | bytes 73736 | tf_op jit(solution)/shard_map/ppermute | solution.py:355
  52.3 3.8 %collective-permute-start.19 = (f32[4,8,128]{2,1,0:T(8,128)S(1)}, f32[4,8,128]{2,1,0:T(8,128)S(1)}, u32[]{:S(2)}, u32[]{:S(2)}) collective-permute-start(f32[4,8,128]{2,1,0:T(8,128)S(1)} %finish.2.mine), channel_id=1, source_target_pairs={{0,8},{8,0},{16,24},{24,16},{1,9},{9,1},{17,25},{25,17},{2,10},{10... | collective-permute-start | bytes 49160 | tf_op jit(solution)/shard_map/ppermute | solution.py:362
  53.9 6.2 %collective-permute-start.18 = (f32[48,128]{1,0:T(8,128)S(1)}, f32[48,128]{1,0:T(8,128)S(1)}, u32[]{:S(2)}, u32[]{:S(2)}) collective-permute-start(f32[48,128]{1,0:T(8,128)S(1)} %merge.8.fwd_mine), channel_id=1, source_target_pairs={{0,1},{1,0},{2,3},{3,2},{4,5},{5,4},{6,7},{7,6},{8,9},{9,8},{10,11... | collective-permute-start | bytes 73736 | tf_op jit(solution)/shard_map/ppermute | solution.py:326
  56.2 3.7 %collective-permute-start.20 = (f32[4,8,128]{2,1,0:T(8,128)S(1)}, f32[4,8,128]{2,1,0:T(8,128)S(1)}, u32[]{:S(2)}, u32[]{:S(2)}) collective-permute-start(f32[4,8,128]{2,1,0:T(8,128)S(1)} %merge.9.mine), channel_id=1, source_target_pairs={{0,16},{8,24},{16,0},{24,8},{1,17},{9,25},{17,1},{25,9},{2,18},{10... | collective-permute-start | bytes 49160 | tf_op jit(solution)/shard_map/ppermute | solution.py:362
  63.2 4.1 %collective-permute-start.21 = (f32[48,128]{1,0:T(8,128)S(1)}, f32[48,128]{1,0:T(8,128)S(1)}, u32[]{:S(2)}, u32[]{:S(2)}) collective-permute-start(f32[48,128]{1,0:T(8,128)S(1)} %get-tuple-element.24.mine), channel_id=1, source_target_pairs={{0,2},{1,3},{2,0},{3,1},{4,6},{5,7},{6,4},{7,5},{8,10},{9,11},{10,... | collective-permute-start | bytes 73736 | tf_op jit(solution)/shard_map/ppermute | solution.py:355
  67.3 4.8 %collective-permute-start.22 = (f32[48,128]{1,0:T(8,128)S(1)}, f32[48,128]{1,0:T(8,128)S(1)}, u32[]{:S(2)}, u32[]{:S(2)}) collective-permute-start(f32[48,128]{1,0:T(8,128)S(1)} %merge.10.mine), channel_id=1, source_target_pairs={{0,4},{1,5},{2,6},{3,7},{4,0},{5,1},{6,2},{7,3},{8,12},{9,13},{10,... | collective-permute-start | bytes 73736 | tf_op jit(solution)/shard_map/ppermute | solution.py:355
  68.2 3.9 %collective-permute-start.24 = (f32[4,8,128]{2,1,0:T(8,128)S(1)}, f32[4,8,128]{2,1,0:T(8,128)S(1)}, u32[]{:S(2)}, u32[]{:S(2)}) collective-permute-start(f32[4,8,128]{2,1,0:T(8,128)S(1)} %finish.3.mine), channel_id=1, source_target_pairs={{0,8},{8,0},{16,24},{24,16},{1,9},{9,1},{17,25},{25,17},{2,10},{10... | collective-permute-start | bytes 49160 | tf_op jit(solution)/shard_map/ppermute | solution.py:362
  72.1 3.9 %collective-permute-start.23 = (f32[48,128]{1,0:T(8,128)S(1)}, f32[48,128]{1,0:T(8,128)S(1)}, u32[]{:S(2)}, u32[]{:S(2)}) collective-permute-start(f32[48,128]{1,0:T(8,128)S(1)} %merge.11.fwd_mine), channel_id=1, source_target_pairs={{0,1},{1,0},{2,3},{3,2},{4,5},{5,4},{6,7},{7,6},{8,9},{9,8},{10,11... | collective-permute-start | bytes 73736 | tf_op jit(solution)/shard_map/ppermute | solution.py:326
  72.2 3.8 %collective-permute-start.25 = (f32[4,8,128]{2,1,0:T(8,128)S(1)}, f32[4,8,128]{2,1,0:T(8,128)S(1)}, u32[]{:S(2)}, u32[]{:S(2)}) collective-permute-start(f32[4,8,128]{2,1,0:T(8,128)S(1)} %merge.12.mine), channel_id=1, source_target_pairs={{0,16},{8,24},{16,0},{24,8},{1,17},{9,25},{17,1},{25,9},{2,18},{10... | collective-permute-start | bytes 49160 | tf_op jit(solution)/shard_map/ppermute | solution.py:362
